TPU v7x, 32 devices: a whole 2x2x4 slice. The times are simulated.
32 devices in a mesh: section: 4 (over x, core), ha: 2 (over y), wa: 4 (over z).
Axes of the slice: x: 2, y: 2, z: 4, core: 2. Of those that a mesh axis runs over, the one named last changes fastest.
Arguments:
- queries: bfloat16 [4, 4, 4, 8, 16, 2560], P('section', None, 'ha', 'wa'), may hold values from -28 to 28
- keys_values: bfloat16 [2, 4, 4, 4, 8, 16, 2560], P(None, 'section', None, 'ha', 'wa'), may hold values from -28 to 28
- grad_out: bfloat16 [4, 4, 4, 8, 16, 2560], P('section', None, 'ha', 'wa'), may hold values from -6 to 6
- time_start: int32 [4, 4, 8], P(None, 'ha', 'wa'), may hold values from 0 to 1, as said below
Outputs:
- grad_qkv: bfloat16 [3, 4, 4, 4, 8, 16, 2560], P(None, 'section', None, 'ha', 'wa')
Inputs may be any that keep to these rules, and one draw needn't show every extreme that they name: Each tile's window begins at most two tiles before the tile and never after it: max(0, t - 2) <= time_start[t, h, w] <= min(t, 1) for time index t.
All inputs are finite; a program needn't handle non-finite values.
Results may differ from a plain program's by a relative error of at most 0.012.
Values may be sent and summed in bfloat16 or wider, within the bound.
A program may use at most 192 MiB of HBM per device.

v0:
```python
import functools

import jax
import jax.numpy as jnp
from jax import lax
from jax.experimental import pallas as pl
from jax.experimental.pallas import tpu as pltpu
from jax.sharding import PartitionSpec as P

HEAD_DIM = 128
HEADS_PER_CHUNK = 1
MESH = pl.DeviceIdType.MESH
F32 = jnp.float32
BF16 = jnp.bfloat16

Y_KV, Z_Q, Z_GO, EXT, CORNER, STAT, DQ, EXT_PART, Y_PART, OUT_Q, OUT_KV, KINDS = 0, 1, 3, 5, 6, 7, 9, 11, 12, 13, 14, 15

AHEAD = 4
CORNERS_AHEAD = 2
STAT_LAG = 2
FOLD_LAG = 4
OUT_LAG = 6
LOW = -1e30


def dot(a, b, contract):
    return lax.dot_general(a, b, ((contract[0], contract[1]), ((), ())), preferred_element_type=F32)


def merge(top, lse, mean, lse_other, mean_other):
    most = jnp.maximum(lse, lse_other)
    w, w_other = jnp.exp(lse - most), jnp.exp(lse_other - most)
    inv = 1.0 / (w + w_other)
    return jnp.exp(top - most) * inv, (w * mean + w_other * mean_other) * inv


def kernel(sizes, starts, q_in, kv_in, go_in, out, q, go, kx, qz, load_sem, first_send, first_recv, first_sem, bias,
           bias_z, e_own, dp_own, st_own, e_z, dp_z, st_z, stat_send, stat_recv, acc, dqa, dqz_send, dqz_recv,
           pz_send, pz_recv, py_send, py_recv, dq, dkv, send_sem, recv_sem):
    n_sec, n_ha, n_wa, chunks, width = sizes
    grid_t, rows, cols, tok, _ = q.shape
    per_col = grid_t * rows * tok
    per_key = grid_t * (rows + 1) * tok
    slots = e_own.shape[0]
    sec, ha, wa = lax.axis_index("section"), lax.axis_index("ha"), lax.axis_index("wa")
    before = lax.rem(sec + n_sec - 1, n_sec)
    after = lax.rem(sec + 1, n_sec)
    other = 1 - ha
    edge = other * (rows - 1)
    has = (wa > 0, wa < n_wa - 1)
    peer = (wa - 1, wa + 1)
    near = (0, cols - 1)
    rim = (wa == 0) | (wa == n_wa - 1)
    by_rim = (wa == 1, wa == n_wa - 2)
    scale = HEAD_DIM ** (-0.5)

    loads = [pltpu.make_async_copy(src, dst, load_sem.at[n]) for n, (src, dst) in enumerate(
        ((q_in, q), (kv_in, kx.at[:, :, 0:rows, 0:cols]), (go_in, go)))]
    barrier = pltpu.get_barrier_semaphore()
    pl.semaphore_signal(barrier, inc=1, device_id=(before, ha, wa), device_id_type=MESH)
    pl.semaphore_signal(barrier, inc=1, device_id=(after, ha, wa), device_id_type=MESH)
    pl.semaphore_signal(barrier, inc=1, device_id=(sec, other, wa), device_id_type=MESH)
    for side in (0, 1):
        @pl.when(has[side])
        def _():
            pl.semaphore_signal(barrier, inc=1, device_id=(sec, ha, peer[side]), device_id_type=MESH)
    pl.semaphore_wait(barrier, 3 + jnp.minimum(wa, 1) + jnp.minimum(n_wa - 1 - wa, 1))

    def keys_move(c):
        return (lax.rem(c, 2) == 1) & (c < chunks - 2)

    def lanes(c):
        return pl.ds(pl.multiple_of(c * width, width), width)

    def channels(c, j):
        return pl.ds(pl.multiple_of(c * width + j * HEAD_DIM, HEAD_DIM), HEAD_DIM)

    def remote(src, dst, sent, arrived, c, device):
        return pltpu.make_async_remote_copy(
            src_ref=src, dst_ref=dst, send_sem=send_sem.at[sent, c], recv_sem=recv_sem.at[arrived, c],
            device_id=device, device_id_type=MESH)

    def y_kv(c):
        return remote(kv_in.at[:, :, edge, :, :, lanes(c)], kx.at[:, :, rows, 0:cols, :, lanes(c)],
                      Y_KV, Y_KV, c, (sec, other, wa))

    class Pair:
        def __init__(self, *copies):
            self.copies = copies

        def start(self):
            for copy in self.copies:
                copy.start()

        def wait_send(self):
            for copy in self.copies:
                copy.wait_send()

        def wait_recv(self):
            for copy in self.copies:
                copy.wait_recv()

    def z_q(side, c, both):
        col = near[side]
        at = slice(0, cols) if both else slice(col, col + 1)
        return Pair(*(
            remote(src.at[:, :, at, :, lanes(c)], qz.at[1 - side, n, :, :, at, :, lanes(c)],
                   kind + side, kind + 1 - side, c, (sec, ha, peer[side]))
            for n, (src, kind) in enumerate(((q_in, Z_Q), (go_in, Z_GO)))))

    def ext(side, c):
        return remote(kv_in.at[:, :, :, near[side], :, lanes(c)], kx.at[:, :, 0:rows, cols, :, lanes(c)],
                      EXT, EXT, c, (sec, ha, peer[side]))

    def corner(side, c):
        return remote(kx.at[:, :, rows, near[side], :, lanes(c)], kx.at[:, :, rows, cols, :, lanes(c)],
                      CORNER, CORNER, c, (sec, ha, peer[side]))

    def stat(side, c, both):
        at = slice(0, per_col * (cols if both else 1))
        return remote(stat_send.at[side, c, :, at], stat_recv.at[1 - side, c, :, at],
                      STAT + side, STAT + 1 - side, c, (sec, ha, peer[side]))

    def dq_back(side, c, both):
        col = near[1 - side]
        at = slice(0, cols) if both else slice(col, col + 1)
        return remote(dqz_send.at[side, :, :, at, :, lanes(c)], dqz_recv.at[1 - side, :, :, at, :, lanes(c)],
                      DQ + side, DQ + 1 - side, c, (sec, ha, peer[side]))

    def ext_part(side, c):
        return remote(pz_send.at[:, :, :, :, lanes(c)], pz_recv.at[:, :, :, :, lanes(c)],
                      EXT_PART, EXT_PART, c, (sec, ha, peer[side]))

    def y_part(c):
        return remote(py_send.at[:, :, :, :, lanes(c)], py_recv.at[:, :, :, :, lanes(c)],
                      Y_PART, Y_PART, c, (sec, other, wa))

    def out_q(c):
        return remote(dq.at[:, :, :, :, lanes(c)], out.at[0, :, :, :, :, lanes(c)],
                      OUT_Q, OUT_Q, c, (before, ha, wa))

    def out_kv(c):
        return remote(dkv.at[:, :, :, :, :, lanes(c)], out.at[pl.ds(1, 2), :, :, :, :, lanes(c)],
                      OUT_KV, OUT_KV, c, (before, ha, wa))

    def if_(cond, action):
        pl.when(cond)(action)

    def leaving(c, action):
        moved = keys_move(c)
        for side in (0, 1):
            if_(has[side] & rim & jnp.logical_not(moved), lambda: action(side, True))
            if_(has[side] & jnp.logical_not(rim), lambda: action(side, False))

    def coming(c, action):
        moved = keys_move(c)
        for side in (0, 1):
            if_(by_rim[side] & jnp.logical_not(moved), lambda: action(side, True))
            if_(has[side] & jnp.logical_not(by_rim[side]), lambda: action(side, False))

    def exchanged(c, action):
        moved = keys_move(c)
        for side in (0, 1):
            wide = (rim | by_rim[side]) & jnp.logical_not(moved)
            if_(has[side] & wide, lambda: action(side, True))
            if_(has[side] & jnp.logical_not(wide), lambda: action(side, False))

    def keys_leave(c, action):
        for side in (0, 1):
            if_(by_rim[side] & keys_move(c), lambda: action(side))

    def keys_come(c, action):
        for side in (0, 1):
            if_(has[side] & rim & keys_move(c), lambda: action(side))

    def stage_send(c):
        y_kv(c).start()
        leaving(c, lambda side, both: z_q(side, c, both).start())
        keys_leave(c, lambda side: ext(side, c).start())

    def passes_corner(c):
        return (by_rim[0] | by_rim[1]) & keys_move(c)

    def stage_corner(c):
        if_(passes_corner(c), lambda: y_kv(c).wait_recv())
        keys_leave(c, lambda side: corner(side, c).start())

    def block(ref, lead, col, ch, n):
        return ref[lead + (slice(None), slice(None), col, slice(None), ch)].reshape(n, HEAD_DIM)

    def joined(ref, lead, at, ch, n):
        return jnp.concatenate([block(ref, lead, col, ch, n) for col in at])

    def first_phase(k, v, qh, gh, bias_of, e_ref, dp_ref, st_ref):
        s = dot(k, qh, ((1,), (1,))) * scale
        s = (s.reshape(-1, per_key, s.shape[1]) + bias_of).reshape(s.shape)
        top = jnp.max(s, axis=0, keepdims=True)
        e = jnp.exp(s - top)
        dp = dot(v, gh, ((1,), (1,)))
        total = jnp.sum(e, axis=0, keepdims=True)
        lse = top + jnp.log(total)
        mean = jnp.sum(e * dp, axis=0, keepdims=True) / total
        e_ref[...] = e
        dp_ref[...] = dp
        st_ref[0:1] = top
        st_ref[1:2] = lse
        st_ref[2:3] = mean
        return lse, mean

    def second_phase(k, qh, gh, e_ref, dp_ref, st_ref, lse_other, mean_other):
        factor, delta = merge(st_ref[0:1], st_ref[1:2], st_ref[2:3], lse_other, mean_other)
        p = e_ref[...] * factor
        ds = (p * (dp_ref[...] - delta)).astype(BF16)
        return (dot(ds, qh, ((1,), (0,))) * scale, dot(p.astype(BF16), gh, ((1,), (0,))),
                dot(ds, k, ((0,), (0,))) * scale)

    def own_first(key_cols, c, j):
        ch, b = channels(c, j), lax.rem(c, slots // HEADS_PER_CHUNK) * HEADS_PER_CHUNK + j
        n = key_cols * per_key
        lse, mean = first_phase(
            joined(kx, (0,), range(key_cols), ch, per_key), joined(kx, (1,), range(key_cols), ch, per_key),
            joined(q, (), range(cols), ch, per_col), joined(go, (), range(cols), ch, per_col),
            bias[...], e_own.at[b, 0:n], dp_own.at[b, 0:n], st_own.at[b])
        for row, value in ((4 * j, lse), (4 * j + 1, mean)):
            for side, order in ((0, (0, 1)), (1, (1, 0))):
                for n, col in enumerate(order):
                    stat_send[side, c, row:row + 1, n * per_col:(n + 1) * per_col] = (
                        value[:, col * per_col:(col + 1) * per_col])

    def own_second(key_cols, c, j):
        ch, b = channels(c, j), lax.rem(c, slots // HEADS_PER_CHUNK) * HEADS_PER_CHUNK + j
        n = key_cols * per_key
        if key_cols > cols:
            lse_other, mean_other = LOW, 0.0
        else:
            def pick(row):
                low = jnp.where(has[0], stat_recv[0, c, row:row + 1, 0:per_col],
                                stat_recv[1, c, row:row + 1, per_col:2 * per_col])
                high = jnp.where(has[1], stat_recv[1, c, row:row + 1, 0:per_col],
                                 stat_recv[0, c, row:row + 1, per_col:2 * per_col])
                return jnp.concatenate([low, high], axis=1)

            lse_other, mean_other = pick(4 * j + 2), pick(4 * j + 3)
        dk, dv, dqh = second_phase(
            joined(kx, (0,), range(key_cols), ch, per_key),
            joined(q, (), range(cols), ch, per_col), joined(go, (), range(cols), ch, per_col),
            e_own.at[b, 0:n], dp_own.at[b, 0:n], st_own.at[b], lse_other, mean_other)
        for i, grad in enumerate((dk, dv)):
            for col in range(key_cols):
                part = grad[col * per_key:(col + 1) * per_key].reshape(grid_t, rows + 1, tok, HEAD_DIM)
                if col < cols:
                    acc[i, :, :, col, :, ch] = part
                else:
                    pz_send[i, :, :, :, ch] = part.astype(BF16)
        for col in range(cols):
            dqa[:, :, col, :, ch] = dqh[col * per_col:(col + 1) * per_col].reshape(grid_t, rows, tok, HEAD_DIM)

    def columns(side, both):
        return (near[1 - side], near[side]) if both else (near[1 - side],)

    def z_first(side, both, c, j):
        ch, b = channels(c, j), lax.rem(c, slots // HEADS_PER_CHUNK) * HEADS_PER_CHUNK + j
        at = columns(side, both)
        n = len(at) * per_col
        lse, mean = first_phase(
            block(kx, (0,), near[side], ch, per_key), block(kx, (1,), near[side], ch, per_key),
            joined(qz, (side, 0), at, ch, per_col), joined(qz, (side, 1), at, ch, per_col),
            bias_z[side, :, 0:n], e_z.at[side, b, :, 0:n], dp_z.at[side, b, :, 0:n], st_z.at[side, b, :, 0:n])
        stat_send[side, c, 4 * j + 2:4 * j + 3, 0:n] = lse
        stat_send[side, c, 4 * j + 3:4 * j + 4, 0:n] = mean

    def z_second(side, both, c, j):
        ch, b = channels(c, j), lax.rem(c, slots // HEADS_PER_CHUNK) * HEADS_PER_CHUNK + j
        at = columns(side, both)
        n = len(at) * per_col
        dk, dv, dqh = second_phase(
            block(kx, (0,), near[side], ch, per_key),
            joined(qz, (side, 0), at, ch, per_col), joined(qz, (side, 1), at, ch, per_col),
            e_z.at[side, b, :, 0:n], dp_z.at[side, b, :, 0:n], st_z.at[side, b, :, 0:n],
            stat_recv[side, c, 4 * j:4 * j + 1, 0:n], stat_recv[side, c, 4 * j + 1:4 * j + 2, 0:n])
        for i, grad in enumerate((dk, dv)):
            acc[i, :, :, near[side], :, ch] += grad.reshape(grid_t, rows + 1, tok, HEAD_DIM)
        for m, col in enumerate(at):
            part = dqh[m * per_col:(m + 1) * per_col].astype(BF16)
            dqz_send[side, :, :, col, :, ch] = part.reshape(grid_t, rows, tok, HEAD_DIM)

    def heads(action):
        for j in range(HEADS_PER_CHUNK):
            action(j)

    def stage_first(c):
        if_(jnp.logical_not(passes_corner(c)), lambda: y_kv(c).wait_recv())

        def arrive(side):
            ext(1 - side, c).wait_recv()
            corner(1 - side, c).wait_recv()

        keys_come(c, arrive)
        far = rim & keys_move(c)
        if_(far, lambda: heads(lambda j: own_first(cols + 1, c, j)))
        if_(jnp.logical_not(far), lambda: heads(lambda j: own_first(cols, c, j)))

        def from_side(side, both):
            z_q(1 - side, c, both).wait_recv()
            heads(lambda j: z_first(side, both, c, j))

        coming(c, from_side)
        exchanged(c, lambda side, both: stat(side, c, both).start())

    def send_y(c):
        py_send[:, :, :, :, lanes(c)] = acc[:, :, rows, :, :, lanes(c)].astype(BF16)
        y_part(c).start()

    def stage_second(c):
        exchanged(c, lambda side, both: stat(1 - side, c, both).wait_recv())
        far = rim & keys_move(c)
        if_(far, lambda: heads(lambda j: own_second(cols + 1, c, j)))
        if_(jnp.logical_not(far), lambda: heads(lambda j: own_second(cols, c, j)))
        keys_come(c, lambda side: ext_part(side, c).start())

        def from_side(side, both):
            heads(lambda j: z_second(side, both, c, j))
            dq_back(side, c, both).start()

        coming(c, from_side)
        if_(jnp.logical_not(passes_corner(c)), lambda: send_y(c))

    def stage_fold(c):
        ch = lanes(c)

        def back(side, both):
            dq_back(1 - side, c, both).wait_recv()
            for col in (range(cols) if both else (near[side],)):
                dqa[:, :, col, :, ch] += dqz_recv[side, :, :, col, :, ch].astype(F32)

        leaving(c, back)
        dq[:, :, :, :, ch] = dqa[:, :, :, :, ch].astype(BF16)
        out_q(c).start()

        def fold(side):
            ext_part(1 - side, c).wait_recv()
            for i in (0, 1):
                acc[i, :, :, near[side], :, ch] += pz_recv[i, :, :, :, ch].astype(F32)

        keys_leave(c, fold)
        if_(passes_corner(c), lambda: send_y(c))

    def stage_out(c):
        ch = lanes(c)
        y_part(c).wait_recv()
        acc[:, :, edge, :, :, ch] += py_recv[:, :, :, :, ch].astype(F32)
        dkv[:, :, :, :, :, ch] = acc[:, :, 0:rows, :, :, ch].astype(BF16)
        out_kv(c).start()

    for c in range(AHEAD):
        stage_send(c)
    for load in loads:
        load.start()

    n_q = cols * per_col
    lane = lax.broadcasted_iota(jnp.int32, (1, n_q), 1)
    first = jnp.zeros((1, n_q), F32)
    for c in range(cols):
        for t in range(grid_t):
            for r in range(rows):
                tile = (c * grid_t + t) * rows + r
                first = jnp.where(lane // tok == tile, starts[r, c, t].astype(F32), first)
    first_send[...] = jnp.broadcast_to(first, first_send.shape)

    def first_copy(side):
        return pltpu.make_async_remote_copy(
            src_ref=first_send, dst_ref=first_recv.at[1 - side], send_sem=first_sem.at[0, side],
            recv_sem=first_sem.at[1, 1 - side], device_id=(sec, ha, peer[side]), device_id_type=MESH)

    for side in (0, 1):
        if_(has[side], lambda: first_copy(side).start())

    def window(ref, begin):
        per_t = (rows + 1) * tok
        for t in range(grid_t):
            seen = (begin <= t) & (begin + 2 >= t)
            row = jnp.where(seen, 0.0, LOW).astype(F32)
            ref[t * per_t:(t + 1) * per_t, :] = jnp.broadcast_to(row, (per_t, n_q))

    window(bias, first)
    for c in range(CORNERS_AHEAD):
        stage_corner(c)
    for side in (0, 1):
        def _(side=side):
            first_copy(1 - side).wait_recv()
            begin = jnp.concatenate(
                [first_recv[side, 0:1, col * per_col:(col + 1) * per_col] for col in columns(side, True)], axis=1)
            window(bias_z.at[side], begin)
        if_(has[side], _)
    for load in loads:
        load.wait()

    def step(i, carry):
        if_(i + AHEAD < chunks, lambda: stage_send(i + AHEAD))
        if_(i + CORNERS_AHEAD < chunks, lambda: stage_corner(i + CORNERS_AHEAD))
        if_(i < chunks, lambda: stage_first(i))
        if_((i >= STAT_LAG) & (i < chunks + STAT_LAG), lambda: stage_second(i - STAT_LAG))
        if_((i >= FOLD_LAG) & (i < chunks + FOLD_LAG), lambda: stage_fold(i - FOLD_LAG))
        if_(i >= OUT_LAG, lambda: stage_out(i - OUT_LAG))
        return carry

    lax.fori_loop(0, chunks + OUT_LAG, step, 0)

    for side in (0, 1):
        if_(has[side], lambda: first_copy(side).wait_send())

    def finish(c, carry):
        y_kv(c).wait_send()
        y_part(c).wait_send()
        leaving(c, lambda side, both: z_q(side, c, both).wait_send())

        def keys_sent(side):
            ext(side, c).wait_send()
            corner(side, c).wait_send()

        keys_leave(c, keys_sent)
        keys_come(c, lambda side: ext_part(side, c).wait_send())
        exchanged(c, lambda side, both: stat(side, c, both).wait_send())
        coming(c, lambda side, both: dq_back(side, c, both).wait_send())
        out_q(c).wait()
        out_kv(c).wait()
        return carry

    lax.fori_loop(0, chunks, finish, 0)


def copy_kernel(src, dst, held, sems):
    parts = [(i, t) for i in range(src.shape[0]) for t in range(src.shape[1])]
    come = [pltpu.make_async_copy(src.at[p], held.at[p], sems.at[0, n]) for n, p in enumerate(parts)]
    go = [pltpu.make_async_copy(held.at[p], dst.at[p], sems.at[1, n]) for n, p in enumerate(parts)]
    for copy in come:
        copy.start()
    for a, b in zip(come, go):
        a.wait()
        b.start()
    for copy in go:
        copy.wait()


def local(mesh_sizes, queries, keys_values, grad_out, time_start):
    n_sec, n_ha, n_wa = mesh_sizes
    q, kv, go = queries[0], keys_values[:, 0], grad_out[0]
    grid_t, rows, cols, tok, channels = q.shape
    assert n_ha == 2 and rows == 2 and cols == 2 and n_wa >= 4 and n_sec >= 2
    width = HEADS_PER_CHUNK * HEAD_DIM
    assert channels % width == 0 and 4 * HEADS_PER_CHUNK <= 8
    chunks = channels // width
    assert chunks >= AHEAD >= CORNERS_AHEAD
    per_col, per_key = grid_t * rows * tok, grid_t * (rows + 1) * tok
    n_q = cols * per_col
    slots = (STAT_LAG + 1) * HEADS_PER_CHUNK
    stay = pl.BlockSpec(memory_space=pl.ANY)
    vmem = pltpu.VMEM
    out = pl.pallas_call(
        functools.partial(kernel, (n_sec, n_ha, n_wa, chunks, width)),
        out_shape=jax.ShapeDtypeStruct((3,) + q.shape, BF16),
        in_specs=[pl.BlockSpec(memory_space=pltpu.SMEM), stay, stay, stay],
        out_specs=pl.BlockSpec(memory_space=pl.ANY),
        scratch_shapes=[
            vmem(q.shape, BF16),
            vmem(go.shape, BF16),
            vmem((2, grid_t, rows + 1, cols + 1, tok, channels), BF16),
            vmem((2, 2) + q.shape, BF16),
            pltpu.SemaphoreType.DMA((3,)),
            vmem((8, n_q), F32),
            vmem((2, 8, n_q), F32),
            pltpu.SemaphoreType.DMA((2, 2)),
            vmem((per_key, n_q), F32),
            vmem((2, per_key, n_q), F32),
            vmem((slots, (cols + 1) * per_key, n_q), F32),
            vmem((slots, (cols + 1) * per_key, n_q), F32),
            vmem((slots, 8, n_q), F32),
            vmem((2, slots, per_key, n_q), F32),
            vmem((2, slots, per_key, n_q), F32),
            vmem((2, slots, 8, n_q), F32),
            vmem((2, chunks, 8, n_q), F32),
            vmem((2, chunks, 8, n_q), F32),
            vmem((2, grid_t, rows + 1, cols, tok, channels), F32),
            vmem(q.shape, F32),
            vmem((2,) + q.shape, BF16),
            vmem((2,) + q.shape, BF16),
            vmem((2, grid_t, rows + 1, tok, channels), BF16),
            vmem((2, grid_t, rows + 1, tok, channels), BF16),
            vmem((2, grid_t, cols, tok, channels), BF16),
            vmem((2, grid_t, cols, tok, channels), BF16),
            vmem(q.shape, BF16),
            vmem((2,) + q.shape, BF16),
            pltpu.SemaphoreType.DMA((KINDS, chunks)),
            pltpu.SemaphoreType.DMA((KINDS, chunks)),
        ],
        compiler_params=pltpu.CompilerParams(
            collective_id=0, has_side_effects=True, vmem_limit_bytes=60 * 1024 * 1024
        ),
    )(time_start.transpose(1, 2, 0), q, kv, go)
    out = pl.pallas_call(
        copy_kernel,
        out_shape=jax.ShapeDtypeStruct(out.shape, BF16),
        in_specs=[pl.BlockSpec(memory_space=pl.ANY)],
        out_specs=pl.BlockSpec(memory_space=pl.ANY),
        scratch_shapes=[pltpu.VMEM(out.shape, BF16), pltpu.SemaphoreType.DMA((2, 3 * grid_t))],
    )(out)
    return out[:, None]


def solution(mesh):
    sizes = (mesh.shape["section"], mesh.shape["ha"], mesh.shape["wa"])
    return jax.shard_map(
        functools.partial(local, sizes),
        mesh=mesh,
        in_specs=(
            P("section", None, "ha", "wa", None, None),
            P(None, "section", None, "ha", "wa", None, None),
            P("section", None, "ha", "wa", None, None),
            P(None, "ha", "wa"),
        ),
        out_specs=P(None, "section", None, "ha", "wa", None, None),
        check_vma=False,
    )
```

profile of v0, /device:TPU:0, one launch (start us, length us, event | category | flops | bytes accessed | tf_op | source)
XLA Modules:
  0.0 98.4 jit_solution(13043706890745381298)
XLA Ops:
  0.0 95.0 %shard_map.46.src = bf16[3,4,2,2,16,2560]{5,4,3,2,1,0:T(8,128)(2,1)} custom-call(s32[2,2,4]{2,1,0:T(2,128)} %bitcast.10, bf16[4,2,2,16,2560]{4,3,2,1,0:T(8,128)(2,1)} %bitcast.8, bf16[2,4,2,2,16,2560]{5,4,3,2,1,0:T(8,128)(2,1)} %bitcast.7, bf16[4,2,2,16,2560]{4,3,2,1,0:T(8,128)(2,1)} %bitcast.9), custom_call_target="tpu_custom_call" | custom-call | tf_op jit(solution)/shard_map/pallas_call | solution.py:459
  95.0 3.5 %shard_map.47 = bf16[3,4,2,2,16,2560]{5,4,3,2,1,0:T(8,128)(2,1)} custom-call(bf16[3,4,2,2,16,2560]{5,4,3,2,1,0:T(8,128)(2,1)} %shard_map.46.src), custom_call_target="tpu_custom_call" | custom-call | tf_op jit(solution)/shard_map/pallas_call | solution.py:500
where the time goes:
time: 99.5 us; the launch traced here: 98.4 us
  Pallas kernels  98.4 us (99%)
    pallas_call x1, Pallas kernels, local(): pl.pallas_call(functools.partial(kernel, (n_sec, n_ha, n_wa, chunks, widt...  95 us
    pallas_call x1, Pallas kernels, local(): pl.pallas_call(copy_kernel, out_shape=jax.ShapeDtypeStruct(out.shape, BF1...  3.47 us

commit v1 on v0

--- a/solution.py
+++ b/solution.py
@@ -15,12 +15,13 @@
 
 Y_KV, Z_Q, Z_GO, EXT, CORNER, STAT, DQ, EXT_PART, Y_PART, OUT_Q, OUT_KV, KINDS = 0, 1, 3, 5, 6, 7, 9, 11, 12, 13, 14, 15
 
-AHEAD = 4
+AHEAD = 3
 CORNERS_AHEAD = 2
 STAT_LAG = 2
 FOLD_LAG = 4
 OUT_LAG = 6
 LOW = -1e30
+VMEM_KIB = 56000
 
 
 def dot(a, b, contract):
@@ -56,6 +57,16 @@
 
     loads = [pltpu.make_async_copy(src, dst, load_sem.at[n]) for n, (src, dst) in enumerate(
         ((q_in, q), (kv_in, kx.at[:, :, 0:rows, 0:cols]), (go_in, go)))]
+    n_q = cols * per_col
+    lane = lax.broadcasted_iota(jnp.int32, (1, n_q), 1)
+    first = jnp.zeros((1, n_q), F32)
+    for c in range(cols):
+        for t in range(grid_t):
+            for r in range(rows):
+                tile = (c * grid_t + t) * rows + r
+                first = jnp.where(lane // tok == tile, starts[r, c, t].astype(F32), first)
+    first_send[...] = jnp.broadcast_to(first, first_send.shape)
+
     barrier = pltpu.get_barrier_semaphore()
     pl.semaphore_signal(barrier, inc=1, device_id=(before, ha, wa), device_id_type=MESH)
     pl.semaphore_signal(barrier, inc=1, device_id=(after, ha, wa), device_id_type=MESH)
@@ -117,7 +128,7 @@
                       CORNER, CORNER, c, (sec, ha, peer[side]))
 
     def stat(side, c, both):
-        at = slice(0, per_col * (cols if both else 1))
+        at = slice(0, cols if both else 1)
         return remote(stat_send.at[side, c, :, at], stat_recv.at[1 - side, c, :, at],
                       STAT + side, STAT + 1 - side, c, (sec, ha, peer[side]))
 
@@ -135,13 +146,12 @@
         return remote(py_send.at[:, :, :, :, lanes(c)], py_recv.at[:, :, :, :, lanes(c)],
                       Y_PART, Y_PART, c, (sec, other, wa))
 
-    def out_q(c):
-        return remote(dq.at[:, :, :, :, lanes(c)], out.at[0, :, :, :, :, lanes(c)],
-                      OUT_Q, OUT_Q, c, (before, ha, wa))
-
-    def out_kv(c):
-        return remote(dkv.at[:, :, :, :, :, lanes(c)], out.at[pl.ds(1, 2), :, :, :, :, lanes(c)],
-                      OUT_KV, OUT_KV, c, (before, ha, wa))
+    def out_q(at):
+        return remote(dq.at[:, :, :, :, at], out.at[0, :, :, :, :, at], OUT_Q, OUT_Q, 0, (before, ha, wa))
+
+    def out_kv(at):
+        return remote(dkv.at[:, :, :, :, :, at], out.at[pl.ds(1, 2), :, :, :, :, at],
+                      OUT_KV, OUT_KV, 0, (before, ha, wa))
 
     def if_(cond, action):
         pl.when(cond)(action)
@@ -221,11 +231,10 @@
             joined(kx, (0,), range(key_cols), ch, per_key), joined(kx, (1,), range(key_cols), ch, per_key),
             joined(q, (), range(cols), ch, per_col), joined(go, (), range(cols), ch, per_col),
             bias[...], e_own.at[b, 0:n], dp_own.at[b, 0:n], st_own.at[b])
-        for row, value in ((4 * j, lse), (4 * j + 1, mean)):
+        for row, value in enumerate((lse, mean)):
             for side, order in ((0, (0, 1)), (1, (1, 0))):
                 for n, col in enumerate(order):
-                    stat_send[side, c, row:row + 1, n * per_col:(n + 1) * per_col] = (
-                        value[:, col * per_col:(col + 1) * per_col])
+                    stat_send[side, c, j, n, row:row + 1] = value[:, col * per_col:(col + 1) * per_col]
 
     def own_second(key_cols, c, j):
         ch, b = channels(c, j), lax.rem(c, slots // HEADS_PER_CHUNK) * HEADS_PER_CHUNK + j
@@ -234,13 +243,12 @@
             lse_other, mean_other = LOW, 0.0
         else:
             def pick(row):
-                low = jnp.where(has[0], stat_recv[0, c, row:row + 1, 0:per_col],
-                                stat_recv[1, c, row:row + 1, per_col:2 * per_col])
-                high = jnp.where(has[1], stat_recv[1, c, row:row + 1, 0:per_col],
-                                 stat_recv[0, c, row:row + 1, per_col:2 * per_col])
+                at = slice(row, row + 1)
+                low = jnp.where(has[0], stat_recv[0, c, j, 0, at], stat_recv[1, c, j, 1, at])
+                high = jnp.where(has[1], stat_recv[1, c, j, 0, at], stat_recv[0, c, j, 1, at])
                 return jnp.concatenate([low, high], axis=1)
 
-            lse_other, mean_other = pick(4 * j + 2), pick(4 * j + 3)
+            lse_other, mean_other = pick(2), pick(3)
         dk, dv, dqh = second_phase(
             joined(kx, (0,), range(key_cols), ch, per_key),
             joined(q, (), range(cols), ch, per_col), joined(go, (), range(cols), ch, per_col),
@@ -266,8 +274,9 @@
             block(kx, (0,), near[side], ch, per_key), block(kx, (1,), near[side], ch, per_key),
             joined(qz, (side, 0), at, ch, per_col), joined(qz, (side, 1), at, ch, per_col),
             bias_z[side, :, 0:n], e_z.at[side, b, :, 0:n], dp_z.at[side, b, :, 0:n], st_z.at[side, b, :, 0:n])
-        stat_send[side, c, 4 * j + 2:4 * j + 3, 0:n] = lse
-        stat_send[side, c, 4 * j + 3:4 * j + 4, 0:n] = mean
+        for row, value in ((2, lse), (3, mean)):
+            for m in range(len(at)):
+                stat_send[side, c, j, m, row:row + 1] = value[:, m * per_col:(m + 1) * per_col]
 
     def z_second(side, both, c, j):
         ch, b = channels(c, j), lax.rem(c, slots // HEADS_PER_CHUNK) * HEADS_PER_CHUNK + j
@@ -277,7 +286,8 @@
             block(kx, (0,), near[side], ch, per_key),
             joined(qz, (side, 0), at, ch, per_col), joined(qz, (side, 1), at, ch, per_col),
             e_z.at[side, b, :, 0:n], dp_z.at[side, b, :, 0:n], st_z.at[side, b, :, 0:n],
-            stat_recv[side, c, 4 * j:4 * j + 1, 0:n], stat_recv[side, c, 4 * j + 1:4 * j + 2, 0:n])
+            *(jnp.concatenate([stat_recv[side, c, j, m, row:row + 1] for m in range(len(at))], axis=1)
+              for row in (0, 1)))
         for i, grad in enumerate((dk, dv)):
             acc[i, :, :, near[side], :, ch] += grad.reshape(grid_t, rows + 1, tok, HEAD_DIM)
         for m, col in enumerate(at):
@@ -335,7 +345,7 @@
 
         leaving(c, back)
         dq[:, :, :, :, ch] = dqa[:, :, :, :, ch].astype(BF16)
-        out_q(c).start()
+        out_q(ch).start()
 
         def fold(side):
             ext_part(1 - side, c).wait_recv()
@@ -344,36 +354,41 @@
 
         keys_leave(c, fold)
         if_(passes_corner(c), lambda: send_y(c))
+
+    def sent(c):
+        y_kv(c).wait_send()
+        y_part(c).wait_send()
+        leaving(c, lambda side, both: z_q(side, c, both).wait_send())
+
+        def keys_sent(side):
+            ext(side, c).wait_send()
+            corner(side, c).wait_send()
+
+        keys_leave(c, keys_sent)
+        keys_come(c, lambda side: ext_part(side, c).wait_send())
+        exchanged(c, lambda side, both: stat(side, c, both).wait_send())
+        coming(c, lambda side, both: dq_back(side, c, both).wait_send())
 
     def stage_out(c):
         ch = lanes(c)
         y_part(c).wait_recv()
         acc[:, :, edge, :, :, ch] += py_recv[:, :, :, :, ch].astype(F32)
         dkv[:, :, :, :, :, ch] = acc[:, :, 0:rows, :, :, ch].astype(BF16)
-        out_kv(c).start()
+        out_kv(ch).start()
+        sent(c)
+
+    def first_copy(side):
+        return pltpu.make_async_remote_copy(
+            src_ref=first_send, dst_ref=first_recv.at[1 - side], send_sem=first_sem.at[0, side],
+            recv_sem=first_sem.at[1, 1 - side], device_id=(sec, ha, peer[side]), device_id_type=MESH)
+
+    for side in (0, 1):
+        if_(has[side], lambda: first_copy(side).start())
 
     for c in range(AHEAD):
         stage_send(c)
     for load in loads:
         load.start()
-
-    n_q = cols * per_col
-    lane = lax.broadcasted_iota(jnp.int32, (1, n_q), 1)
-    first = jnp.zeros((1, n_q), F32)
-    for c in range(cols):
-        for t in range(grid_t):
-            for r in range(rows):
-                tile = (c * grid_t + t) * rows + r
-                first = jnp.where(lane // tok == tile, starts[r, c, t].astype(F32), first)
-    first_send[...] = jnp.broadcast_to(first, first_send.shape)
-
-    def first_copy(side):
-        return pltpu.make_async_remote_copy(
-            src_ref=first_send, dst_ref=first_recv.at[1 - side], send_sem=first_sem.at[0, side],
-            recv_sem=first_sem.at[1, 1 - side], device_id=(sec, ha, peer[side]), device_id_type=MESH)
-
-    for side in (0, 1):
-        if_(has[side], lambda: first_copy(side).start())
 
     def window(ref, begin):
         per_t = (rows + 1) * tok
@@ -409,37 +424,8 @@
     for side in (0, 1):
         if_(has[side], lambda: first_copy(side).wait_send())
 
-    def finish(c, carry):
-        y_kv(c).wait_send()
-        y_part(c).wait_send()
-        leaving(c, lambda side, both: z_q(side, c, both).wait_send())
-
-        def keys_sent(side):
-            ext(side, c).wait_send()
-            corner(side, c).wait_send()
-
-        keys_leave(c, keys_sent)
-        keys_come(c, lambda side: ext_part(side, c).wait_send())
-        exchanged(c, lambda side, both: stat(side, c, both).wait_send())
-        coming(c, lambda side, both: dq_back(side, c, both).wait_send())
-        out_q(c).wait()
-        out_kv(c).wait()
-        return carry
-
-    lax.fori_loop(0, chunks, finish, 0)
-
-
-def copy_kernel(src, dst, held, sems):
-    parts = [(i, t) for i in range(src.shape[0]) for t in range(src.shape[1])]
-    come = [pltpu.make_async_copy(src.at[p], held.at[p], sems.at[0, n]) for n, p in enumerate(parts)]
-    go = [pltpu.make_async_copy(held.at[p], dst.at[p], sems.at[1, n]) for n, p in enumerate(parts)]
-    for copy in come:
-        copy.start()
-    for a, b in zip(come, go):
-        a.wait()
-        b.start()
-    for copy in go:
-        copy.wait()
+    out_q(slice(None)).wait()
+    out_kv(slice(None)).wait()
 
 
 def local(mesh_sizes, queries, keys_values, grad_out, time_start):
@@ -448,7 +434,7 @@
     grid_t, rows, cols, tok, channels = q.shape
     assert n_ha == 2 and rows == 2 and cols == 2 and n_wa >= 4 and n_sec >= 2
     width = HEADS_PER_CHUNK * HEAD_DIM
-    assert channels % width == 0 and 4 * HEADS_PER_CHUNK <= 8
+    assert channels % width == 0
     chunks = channels // width
     assert chunks >= AHEAD >= CORNERS_AHEAD
     per_col, per_key = grid_t * rows * tok, grid_t * (rows + 1) * tok
@@ -458,9 +444,9 @@
     vmem = pltpu.VMEM
     out = pl.pallas_call(
         functools.partial(kernel, (n_sec, n_ha, n_wa, chunks, width)),
-        out_shape=jax.ShapeDtypeStruct((3,) + q.shape, BF16),
+        out_shape=pltpu.VMEM((3,) + q.shape, BF16),
         in_specs=[pl.BlockSpec(memory_space=pltpu.SMEM), stay, stay, stay],
-        out_specs=pl.BlockSpec(memory_space=pl.ANY),
+        out_specs=pl.BlockSpec(memory_space=pltpu.VMEM),
         scratch_shapes=[
             vmem(q.shape, BF16),
             vmem(go.shape, BF16),
@@ -478,8 +464,8 @@
             vmem((2, slots, per_key, n_q), F32),
             vmem((2, slots, per_key, n_q), F32),
             vmem((2, slots, 8, n_q), F32),
-            vmem((2, chunks, 8, n_q), F32),
-            vmem((2, chunks, 8, n_q), F32),
+            vmem((2, chunks, HEADS_PER_CHUNK, cols, 4, per_col), F32),
+            vmem((2, chunks, HEADS_PER_CHUNK, cols, 4, per_col), F32),
             vmem((2, grid_t, rows + 1, cols, tok, channels), F32),
             vmem(q.shape, F32),
             vmem((2,) + q.shape, BF16),
@@ -494,16 +480,9 @@
             pltpu.SemaphoreType.DMA((KINDS, chunks)),
         ],
         compiler_params=pltpu.CompilerParams(
-            collective_id=0, has_side_effects=True, vmem_limit_bytes=60 * 1024 * 1024
+            collective_id=0, has_side_effects=True, vmem_limit_bytes=VMEM_KIB * 1024
         ),
     )(time_start.transpose(1, 2, 0), q, kv, go)
-    out = pl.pallas_call(
-        copy_kernel,
-        out_shape=jax.ShapeDtypeStruct(out.shape, BF16),
-        in_specs=[pl.BlockSpec(memory_space=pl.ANY)],
-        out_specs=pl.BlockSpec(memory_space=pl.ANY),
-        scratch_shapes=[pltpu.VMEM(out.shape, BF16), pltpu.SemaphoreType.DMA((2, 3 * grid_t))],
-    )(out)
     return out[:, None]
 
 

time: 99.5 us -> 93.1 us (0.936)
  Pallas kernels: 98.4 us -> 89.5 us
  local copies, waits for them, and re-layouts: 0 us -> 1.93 us
    pallas_call x1, Pallas kernels: 95 us -> 89.5 us  [local(): pl.pallas_call(functools.partial(kernel, (n_sec, n_ha, n_wa, chunks, widt...]
    pallas_call x1 -> x0, Pallas kernels: 3.47 us -> none  [local(): pl.pallas_call(copy_kernel, out_shape=jax.ShapeDtypeStruct(out.shape, BF1...]
    unnamed x0 -> x1, local copies, waits for them, and re-layouts: none -> 1.93 us
where the time goes in v1:
time: 93.1 us; the launch traced here: 91.5 us
  Pallas kernels  89.5 us (96%)
  local copies, waits for them, and re-layouts  1.93 us (2%)
    pallas_call x1, Pallas kernels, local(): pl.pallas_call(functools.partial(kernel, (n_sec, n_ha, n_wa, chunks, widt...  89.5 us
    unnamed x1, local copies, waits for them, and re-layouts  1.93 us

profile of v1, /device:TPU:0, one launch (start us, length us, event | category | flops | bytes accessed | tf_op | source)
XLA Modules:
  0.0 91.5 jit_solution(11227426690441937706)
XLA Ops:
  0.0 89.5 %shard_map.46 = bf16[3,4,2,2,16,2560]{5,4,3,2,1,0:T(8,128)(2,1)S(1)} custom-call(s32[2,2,4]{2,1,0:T(2,128)} %bitcast.11, bf16[4,2,2,16,2560]{4,3,2,1,0:T(8,128)(2,1)} %bitcast.9, bf16[2,4,2,2,16,2560]{5,4,3,2,1,0:T(8,128)(2,1)} %bitcast.8, bf16[4,2,2,16,2560]{4,3,2,1,0:T(8,128)(2,1)} %bitcast.10), custom_call_target="tpu_custom_call" | custom-call | tf_op jit(solution)/shard_map/pallas_call | solution.py:445
  89.5 1.9 %copy.7 = bf16[3,1,4,2,2,16,2560]{6,5,4,3,2,1,0:T(8,128)(2,1)} copy(bf16[3,1,4,2,2,16,2560]{6,5,4,3,2,1,0:T(8,128)(2,1)S(1)} %bitcast.7) | data formatting | bytes 7864320

commit v2 on v1

--- a/solution.py
+++ b/solution.py
@@ -13,13 +13,15 @@
 F32 = jnp.float32
 BF16 = jnp.bfloat16
 
-Y_KV, Z_Q, Z_GO, EXT, CORNER, STAT, DQ, EXT_PART, Y_PART, OUT_Q, OUT_KV, KINDS = 0, 1, 3, 5, 6, 7, 9, 11, 12, 13, 14, 15
-
-AHEAD = 3
+Y_KV, Z_Q, EXT, CORNER, STAT, DQ, EXT_PART, CORNER_PART, Y_PART, OUT, KINDS = (
+    0, 1, 3, 4, 5, 7, 9, 10, 11, 12, 13)
+
+AHEAD_Y = 5
+AHEAD_Q = 3
+AHEAD_E = 3
 CORNERS_AHEAD = 2
 STAT_LAG = 2
 FOLD_LAG = 4
-OUT_LAG = 6
 LOW = -1e30
 VMEM_KIB = 56000
 
@@ -35,11 +37,11 @@
     return jnp.exp(top - most) * inv, (w * mean + w_other * mean_other) * inv
 
 
-def kernel(sizes, starts, q_in, kv_in, go_in, out, q, go, kx, qz, load_sem, first_send, first_recv, first_sem, bias,
-           bias_z, e_own, dp_own, st_own, e_z, dp_z, st_z, stat_send, stat_recv, acc, dqa, dqz_send, dqz_recv,
-           pz_send, pz_recv, py_send, py_recv, dq, dkv, send_sem, recv_sem):
+def kernel(sizes, starts, q_in, kv_in, go_in, out, qg, kx, qz, load_sem, first_send, first_recv, first_sem, bias,
+           bias_z, e_own, dp_own, st_own, e_z, dp_z, st_z, stat_send, stat_recv, acc, dqz_send, dqz_recv,
+           pz_send, pz_recv, pc_recv, py_send, py_recv, own, total, send_sem, recv_sem):
     n_sec, n_ha, n_wa, chunks, width = sizes
-    grid_t, rows, cols, tok, _ = q.shape
+    _, grid_t, rows, cols, tok, _ = qg.shape
     per_col = grid_t * rows * tok
     per_key = grid_t * (rows + 1) * tok
     slots = e_own.shape[0]
@@ -56,7 +58,10 @@
     scale = HEAD_DIM ** (-0.5)
 
     loads = [pltpu.make_async_copy(src, dst, load_sem.at[n]) for n, (src, dst) in enumerate(
-        ((q_in, q), (kv_in, kx.at[:, :, 0:rows, 0:cols]), (go_in, go)))]
+        ((q_in, qg.at[0]), (go_in, qg.at[1]), (kv_in, kx.at[:, :, 0:rows, 0:cols])))]
+    for load in loads:
+        load.start()
+
     n_q = cols * per_col
     lane = lax.broadcasted_iota(jnp.int32, (1, n_q), 1)
     first = jnp.zeros((1, n_q), F32)
@@ -68,20 +73,34 @@
     first_send[...] = jnp.broadcast_to(first, first_send.shape)
 
     barrier = pltpu.get_barrier_semaphore()
-    pl.semaphore_signal(barrier, inc=1, device_id=(before, ha, wa), device_id_type=MESH)
-    pl.semaphore_signal(barrier, inc=1, device_id=(after, ha, wa), device_id_type=MESH)
-    pl.semaphore_signal(barrier, inc=1, device_id=(sec, other, wa), device_id_type=MESH)
+
+    def greet(*device):
+        pl.semaphore_signal(barrier, inc=1, device_id=device, device_id_type=MESH)
+
+    greet(before, ha, wa)
+    greet(after, ha, wa)
+    greet(sec, other, wa)
     for side in (0, 1):
         @pl.when(has[side])
         def _():
-            pl.semaphore_signal(barrier, inc=1, device_id=(sec, ha, peer[side]), device_id_type=MESH)
-    pl.semaphore_wait(barrier, 3 + jnp.minimum(wa, 1) + jnp.minimum(n_wa - 1 - wa, 1))
+            greet(sec, ha, peer[side])
+
+        @pl.when(has[side] & (rim | by_rim[side]))
+        def _():
+            greet(sec, other, peer[side])
+
+    sides_here = jnp.minimum(wa, 1) + jnp.minimum(n_wa - 1 - wa, 1)
+    rims_here = jnp.where(rim, 1, by_rim[0].astype(jnp.int32) + by_rim[1].astype(jnp.int32))
+    pl.semaphore_wait(barrier, 3 + sides_here + rims_here)
 
     def keys_move(c):
-        return (lax.rem(c, 2) == 1) & (c < chunks - 2)
+        return ((lax.rem(c, 5) == 2) | (lax.rem(c, 5) == 0)) & (c > 0) & (c < chunks - 2)
 
     def lanes(c):
         return pl.ds(pl.multiple_of(c * width, width), width)
+
+    def within(j):
+        return slice(j * HEAD_DIM, (j + 1) * HEAD_DIM)
 
     def channels(c, j):
         return pl.ds(pl.multiple_of(c * width + j * HEAD_DIM, HEAD_DIM), HEAD_DIM)
@@ -92,35 +111,16 @@
             device_id=device, device_id_type=MESH)
 
     def y_kv(c):
-        return remote(kv_in.at[:, :, edge, :, :, lanes(c)], kx.at[:, :, rows, 0:cols, :, lanes(c)],
+        return remote(kx.at[:, :, edge, 0:cols, :, lanes(c)], kx.at[:, :, rows, 0:cols, :, lanes(c)],
                       Y_KV, Y_KV, c, (sec, other, wa))
 
-    class Pair:
-        def __init__(self, *copies):
-            self.copies = copies
-
-        def start(self):
-            for copy in self.copies:
-                copy.start()
-
-        def wait_send(self):
-            for copy in self.copies:
-                copy.wait_send()
-
-        def wait_recv(self):
-            for copy in self.copies:
-                copy.wait_recv()
-
     def z_q(side, c, both):
-        col = near[side]
-        at = slice(0, cols) if both else slice(col, col + 1)
-        return Pair(*(
-            remote(src.at[:, :, at, :, lanes(c)], qz.at[1 - side, n, :, :, at, :, lanes(c)],
-                   kind + side, kind + 1 - side, c, (sec, ha, peer[side]))
-            for n, (src, kind) in enumerate(((q_in, Z_Q), (go_in, Z_GO)))))
+        at = slice(0, cols) if both else slice(near[side], near[side] + 1)
+        return remote(qg.at[:, :, :, at, :, lanes(c)], qz.at[1 - side, :, :, :, at, :, lanes(c)],
+                      Z_Q + side, Z_Q + 1 - side, c, (sec, ha, peer[side]))
 
     def ext(side, c):
-        return remote(kv_in.at[:, :, :, near[side], :, lanes(c)], kx.at[:, :, 0:rows, cols, :, lanes(c)],
+        return remote(kx.at[:, :, 0:rows, near[side], :, lanes(c)], kx.at[:, :, 0:rows, cols, :, lanes(c)],
                       EXT, EXT, c, (sec, ha, peer[side]))
 
     def corner(side, c):
@@ -139,19 +139,19 @@
                       DQ + side, DQ + 1 - side, c, (sec, ha, peer[side]))
 
     def ext_part(side, c):
-        return remote(pz_send.at[:, :, :, :, lanes(c)], pz_recv.at[:, :, :, :, lanes(c)],
+        return remote(pz_send.at[:, :, 0:rows, :, lanes(c)], pz_recv.at[:, :, :, :, lanes(c)],
                       EXT_PART, EXT_PART, c, (sec, ha, peer[side]))
+
+    def corner_part(side, c):
+        return remote(pz_send.at[:, :, rows, :, lanes(c)], pc_recv.at[:, :, :, lanes(c)],
+                      CORNER_PART, CORNER_PART, c, (sec, other, peer[side]))
 
     def y_part(c):
         return remote(py_send.at[:, :, :, :, lanes(c)], py_recv.at[:, :, :, :, lanes(c)],
                       Y_PART, Y_PART, c, (sec, other, wa))
 
-    def out_q(at):
-        return remote(dq.at[:, :, :, :, at], out.at[0, :, :, :, :, at], OUT_Q, OUT_Q, 0, (before, ha, wa))
-
-    def out_kv(at):
-        return remote(dkv.at[:, :, :, :, :, at], out.at[pl.ds(1, 2), :, :, :, :, at],
-                      OUT_KV, OUT_KV, 0, (before, ha, wa))
+    def result(at):
+        return remote(own.at[:, :, :, :, :, at], out.at[:, :, :, :, :, at], OUT, OUT, 0, (before, ha, wa))
 
     def if_(cond, action):
         pl.when(cond)(action)
@@ -183,10 +183,13 @@
         for side in (0, 1):
             if_(has[side] & rim & keys_move(c), lambda: action(side))
 
-    def stage_send(c):
-        y_kv(c).start()
-        leaving(c, lambda side, both: z_q(side, c, both).start())
-        keys_leave(c, lambda side: ext(side, c).start())
+    def stage_send(c, y, z, keys):
+        if y:
+            y_kv(c).start()
+        if z:
+            leaving(c, lambda side, both: z_q(side, c, both).start())
+        if keys:
+            keys_leave(c, lambda side: ext(side, c).start())
 
     def passes_corner(c):
         return (by_rim[0] | by_rim[1]) & keys_move(c)
@@ -229,7 +232,7 @@
         n = key_cols * per_key
         lse, mean = first_phase(
             joined(kx, (0,), range(key_cols), ch, per_key), joined(kx, (1,), range(key_cols), ch, per_key),
-            joined(q, (), range(cols), ch, per_col), joined(go, (), range(cols), ch, per_col),
+            joined(qg, (0,), range(cols), ch, per_col), joined(qg, (1,), range(cols), ch, per_col),
             bias[...], e_own.at[b, 0:n], dp_own.at[b, 0:n], st_own.at[b])
         for row, value in enumerate((lse, mean)):
             for side, order in ((0, (0, 1)), (1, (1, 0))):
@@ -251,17 +254,18 @@
             lse_other, mean_other = pick(2), pick(3)
         dk, dv, dqh = second_phase(
             joined(kx, (0,), range(key_cols), ch, per_key),
-            joined(q, (), range(cols), ch, per_col), joined(go, (), range(cols), ch, per_col),
+            joined(qg, (0,), range(cols), ch, per_col), joined(qg, (1,), range(cols), ch, per_col),
             e_own.at[b, 0:n], dp_own.at[b, 0:n], st_own.at[b], lse_other, mean_other)
         for i, grad in enumerate((dk, dv)):
             for col in range(key_cols):
                 part = grad[col * per_key:(col + 1) * per_key].reshape(grid_t, rows + 1, tok, HEAD_DIM)
                 if col < cols:
-                    acc[i, :, :, col, :, ch] = part
+                    acc[i, :, :, col, :, within(j)] = part
                 else:
                     pz_send[i, :, :, :, ch] = part.astype(BF16)
         for col in range(cols):
-            dqa[:, :, col, :, ch] = dqh[col * per_col:(col + 1) * per_col].reshape(grid_t, rows, tok, HEAD_DIM)
+            part = dqh[col * per_col:(col + 1) * per_col].astype(BF16)
+            own[0, :, :, col, :, ch] = part.reshape(grid_t, rows, tok, HEAD_DIM)
 
     def columns(side, both):
         return (near[1 - side], near[side]) if both else (near[1 - side],)
@@ -289,7 +293,7 @@
             *(jnp.concatenate([stat_recv[side, c, j, m, row:row + 1] for m in range(len(at))], axis=1)
               for row in (0, 1)))
         for i, grad in enumerate((dk, dv)):
-            acc[i, :, :, near[side], :, ch] += grad.reshape(grid_t, rows + 1, tok, HEAD_DIM)
+            acc[i, :, :, near[side], :, within(j)] += grad.reshape(grid_t, rows + 1, tok, HEAD_DIM)
         for m, col in enumerate(at):
             part = dqh[m * per_col:(m + 1) * per_col].astype(BF16)
             dqz_send[side, :, :, col, :, ch] = part.reshape(grid_t, rows, tok, HEAD_DIM)
@@ -316,65 +320,70 @@
 
         coming(c, from_side)
         exchanged(c, lambda side, both: stat(side, c, both).start())
-
-    def send_y(c):
-        py_send[:, :, :, :, lanes(c)] = acc[:, :, rows, :, :, lanes(c)].astype(BF16)
-        y_part(c).start()
 
     def stage_second(c):
         exchanged(c, lambda side, both: stat(1 - side, c, both).wait_recv())
         far = rim & keys_move(c)
         if_(far, lambda: heads(lambda j: own_second(cols + 1, c, j)))
         if_(jnp.logical_not(far), lambda: heads(lambda j: own_second(cols, c, j)))
-        keys_come(c, lambda side: ext_part(side, c).start())
+
+        def extra(side):
+            ext_part(side, c).start()
+            corner_part(side, c).start()
+
+        keys_come(c, extra)
 
         def from_side(side, both):
             heads(lambda j: z_second(side, both, c, j))
             dq_back(side, c, both).start()
 
         coming(c, from_side)
-        if_(jnp.logical_not(passes_corner(c)), lambda: send_y(c))
+        ch = lanes(c)
+        py_send[:, :, :, :, ch] = acc[:, :, rows].astype(BF16)
+        y_part(c).start()
+        own[1:3, :, :, :, :, ch] = acc[:, :, 0:rows].astype(BF16)
+
+    def sent(c):
+        y_kv(c).wait_send()
+        leaving(c, lambda side, both: z_q(side, c, both).wait_send())
+
+        def keys_sent(side):
+            ext(side, c).wait_send()
+            corner(side, c).wait_send()
+
+        keys_leave(c, keys_sent)
+
+        def extra_sent(side):
+            ext_part(side, c).wait_send()
+            corner_part(side, c).wait_send()
+
+        keys_come(c, extra_sent)
+        exchanged(c, lambda side, both: stat(side, c, both).wait_send())
+        coming(c, lambda side, both: dq_back(side, c, both).wait_send())
+        y_part(c).wait_send()
 
     def stage_fold(c):
         ch = lanes(c)
+        total[...] = own[:, :, :, :, :, ch].astype(F32)
+
+        def fold(side):
+            ext_part(1 - side, c).wait_recv()
+            corner_part(1 - side, c).wait_recv()
+            total[1:3, :, :, near[side]] += pz_recv[:, :, :, :, ch].astype(F32)
+            total[1:3, :, edge, near[side]] += pc_recv[:, :, :, ch].astype(F32)
+
+        keys_leave(c, fold)
+        y_part(c).wait_recv()
+        total[1:3, :, edge] += py_recv[:, :, :, :, ch].astype(F32)
 
         def back(side, both):
             dq_back(1 - side, c, both).wait_recv()
             for col in (range(cols) if both else (near[side],)):
-                dqa[:, :, col, :, ch] += dqz_recv[side, :, :, col, :, ch].astype(F32)
+                total[0, :, :, col] += dqz_recv[side, :, :, col, :, ch].astype(F32)
 
         leaving(c, back)
-        dq[:, :, :, :, ch] = dqa[:, :, :, :, ch].astype(BF16)
-        out_q(ch).start()
-
-        def fold(side):
-            ext_part(1 - side, c).wait_recv()
-            for i in (0, 1):
-                acc[i, :, :, near[side], :, ch] += pz_recv[i, :, :, :, ch].astype(F32)
-
-        keys_leave(c, fold)
-        if_(passes_corner(c), lambda: send_y(c))
-
-    def sent(c):
-        y_kv(c).wait_send()
-        y_part(c).wait_send()
-        leaving(c, lambda side, both: z_q(side, c, both).wait_send())
-
-        def keys_sent(side):
-            ext(side, c).wait_send()
-            corner(side, c).wait_send()
-
-        keys_leave(c, keys_sent)
-        keys_come(c, lambda side: ext_part(side, c).wait_send())
-        exchanged(c, lambda side, both: stat(side, c, both).wait_send())
-        coming(c, lambda side, both: dq_back(side, c, both).wait_send())
-
-    def stage_out(c):
-        ch = lanes(c)
-        y_part(c).wait_recv()
-        acc[:, :, edge, :, :, ch] += py_recv[:, :, :, :, ch].astype(F32)
-        dkv[:, :, :, :, :, ch] = acc[:, :, 0:rows, :, :, ch].astype(BF16)
-        out_kv(ch).start()
+        own[:, :, :, :, :, ch] = total[...].astype(BF16)
+        result(ch).start()
         sent(c)
 
     def first_copy(side):
@@ -385,10 +394,10 @@
     for side in (0, 1):
         if_(has[side], lambda: first_copy(side).start())
 
-    for c in range(AHEAD):
-        stage_send(c)
     for load in loads:
-        load.start()
+        load.wait()
+    for c in range(max(AHEAD_Y, AHEAD_Q, AHEAD_E)):
+        stage_send(c, c < AHEAD_Y, c < AHEAD_Q, c < AHEAD_E)
 
     def window(ref, begin):
         per_t = (rows + 1) * tok
@@ -407,25 +416,21 @@
                 [first_recv[side, 0:1, col * per_col:(col + 1) * per_col] for col in columns(side, True)], axis=1)
             window(bias_z.at[side], begin)
         if_(has[side], _)
-    for load in loads:
-        load.wait()
 
     def step(i, carry):
-        if_(i + AHEAD < chunks, lambda: stage_send(i + AHEAD))
+        if_(i + AHEAD_Y < chunks, lambda: stage_send(i + AHEAD_Y, True, False, False))
+        if_(i + AHEAD_Q < chunks, lambda: stage_send(i + AHEAD_Q, False, True, False))
+        if_(i + AHEAD_E < chunks, lambda: stage_send(i + AHEAD_E, False, False, True))
         if_(i + CORNERS_AHEAD < chunks, lambda: stage_corner(i + CORNERS_AHEAD))
         if_(i < chunks, lambda: stage_first(i))
         if_((i >= STAT_LAG) & (i < chunks + STAT_LAG), lambda: stage_second(i - STAT_LAG))
-        if_((i >= FOLD_LAG) & (i < chunks + FOLD_LAG), lambda: stage_fold(i - FOLD_LAG))
-        if_(i >= OUT_LAG, lambda: stage_out(i - OUT_LAG))
+        if_(i >= FOLD_LAG, lambda: stage_fold(i - FOLD_LAG))
         return carry
 
-    lax.fori_loop(0, chunks + OUT_LAG, step, 0)
-
+    lax.fori_loop(0, chunks + FOLD_LAG, step, 0)
+    result(slice(None)).wait()
     for side in (0, 1):
         if_(has[side], lambda: first_copy(side).wait_send())
-
-    out_q(slice(None)).wait()
-    out_kv(slice(None)).wait()
 
 
 def local(mesh_sizes, queries, keys_values, grad_out, time_start):
@@ -436,7 +441,7 @@
     width = HEADS_PER_CHUNK * HEAD_DIM
     assert channels % width == 0
     chunks = channels // width
-    assert chunks >= AHEAD >= CORNERS_AHEAD
+    assert chunks >= max(AHEAD_Y, AHEAD_Q, AHEAD_E) and AHEAD_Y >= CORNERS_AHEAD
     per_col, per_key = grid_t * rows * tok, grid_t * (rows + 1) * tok
     n_q = cols * per_col
     slots = (STAT_LAG + 1) * HEADS_PER_CHUNK
@@ -448,8 +453,7 @@
         in_specs=[pl.BlockSpec(memory_space=pltpu.SMEM), stay, stay, stay],
         out_specs=pl.BlockSpec(memory_space=pltpu.VMEM),
         scratch_shapes=[
-            vmem(q.shape, BF16),
-            vmem(go.shape, BF16),
+            vmem((2,) + q.shape, BF16),
             vmem((2, grid_t, rows + 1, cols + 1, tok, channels), BF16),
             vmem((2, 2) + q.shape, BF16),
             pltpu.SemaphoreType.DMA((3,)),
@@ -466,16 +470,16 @@
             vmem((2, slots, 8, n_q), F32),
             vmem((2, chunks, HEADS_PER_CHUNK, cols, 4, per_col), F32),
             vmem((2, chunks, HEADS_PER_CHUNK, cols, 4, per_col), F32),
-            vmem((2, grid_t, rows + 1, cols, tok, channels), F32),
-            vmem(q.shape, F32),
+            vmem((2, grid_t, rows + 1, cols, tok, width), F32),
             vmem((2,) + q.shape, BF16),
             vmem((2,) + q.shape, BF16),
             vmem((2, grid_t, rows + 1, tok, channels), BF16),
-            vmem((2, grid_t, rows + 1, tok, channels), BF16),
+            vmem((2, grid_t, rows, tok, channels), BF16),
+            vmem((2, grid_t, tok, channels), BF16),
             vmem((2, grid_t, cols, tok, channels), BF16),
             vmem((2, grid_t, cols, tok, channels), BF16),
-            vmem(q.shape, BF16),
-            vmem((2,) + q.shape, BF16),
+            vmem((3,) + q.shape, BF16),
+            vmem((3, grid_t, rows, cols, tok, width), F32),
             pltpu.SemaphoreType.DMA((KINDS, chunks)),
             pltpu.SemaphoreType.DMA((KINDS, chunks)),
         ],

time: 93.1 us -> 88.7 us (0.953)
  the two profiles are of different devices: /device:TPU:0 before, /device:TPU:17 now
where the time goes in v2:
time: 88.7 us; the launch traced here: 88.6 us
  Pallas kernels  86.6 us (98%)
  local copies, waits for them, and re-layouts  1.93 us (2%)
    pallas_call x1, Pallas kernels, local(): pl.pallas_call(functools.partial(kernel, (n_sec, n_ha, n_wa, chunks, widt...  86.6 us
    unnamed x1, local copies, waits for them, and re-layouts  1.93 us

profile of v2, /device:TPU:17, one launch (start us, length us, event | category | flops | bytes accessed | tf_op | source)
XLA Modules:
  0.0 88.6 jit_solution(13559240141577907133)
XLA Ops:
  0.0 86.6 %shard_map.46 = bf16[3,4,2,2,16,2560]{5,4,3,2,1,0:T(8,128)(2,1)S(1)} custom-call(s32[2,2,4]{2,1,0:T(2,128)} %bitcast.11, bf16[4,2,2,16,2560]{4,3,2,1,0:T(8,128)(2,1)} %bitcast.9, bf16[2,4,2,2,16,2560]{5,4,3,2,1,0:T(8,128)(2,1)} %bitcast.8, bf16[4,2,2,16,2560]{4,3,2,1,0:T(8,128)(2,1)} %bitcast.10), custom_call_target="tpu_custom_call" | custom-call | tf_op jit(solution)/shard_map/pallas_call | solution.py:450
  86.7 1.9 %copy.7 = bf16[3,1,4,2,2,16,2560]{6,5,4,3,2,1,0:T(8,128)(2,1)} copy(bf16[3,1,4,2,2,16,2560]{6,5,4,3,2,1,0:T(8,128)(2,1)S(1)} %bitcast.7) | data formatting | bytes 7864320

commit v3 on v2

--- a/solution.py
+++ b/solution.py
@@ -16,9 +16,9 @@
 Y_KV, Z_Q, EXT, CORNER, STAT, DQ, EXT_PART, CORNER_PART, Y_PART, OUT, KINDS = (
     0, 1, 3, 4, 5, 7, 9, 10, 11, 12, 13)
 
-AHEAD_Y = 5
-AHEAD_Q = 3
-AHEAD_E = 3
+AHEAD_Y = 6
+AHEAD_Q = 3, 3
+AHEAD_E = 3, 3
 CORNERS_AHEAD = 2
 STAT_LAG = 2
 FOLD_LAG = 4
@@ -39,7 +39,7 @@
 
 def kernel(sizes, starts, q_in, kv_in, go_in, out, qg, kx, qz, load_sem, first_send, first_recv, first_sem, bias,
            bias_z, e_own, dp_own, st_own, e_z, dp_z, st_z, stat_send, stat_recv, acc, dqz_send, dqz_recv,
-           pz_send, pz_recv, pc_recv, py_send, py_recv, own, total, send_sem, recv_sem):
+           pz_send, pz_recv, pc_recv, py_send, py_recv, own, total_q, total_kv, send_sem, recv_sem):
     n_sec, n_ha, n_wa, chunks, width = sizes
     _, grid_t, rows, cols, tok, _ = qg.shape
     per_col = grid_t * rows * tok
@@ -50,6 +50,7 @@
     after = lax.rem(sec + 1, n_sec)
     other = 1 - ha
     edge = other * (rows - 1)
+    inner = rows - 1 - edge
     has = (wa > 0, wa < n_wa - 1)
     peer = (wa - 1, wa + 1)
     near = (0, cols - 1)
@@ -150,8 +151,11 @@
         return remote(py_send.at[:, :, :, :, lanes(c)], py_recv.at[:, :, :, :, lanes(c)],
                       Y_PART, Y_PART, c, (sec, other, wa))
 
-    def result(at):
-        return remote(own.at[:, :, :, :, :, at], out.at[:, :, :, :, :, at], OUT, OUT, 0, (before, ha, wa))
+    def result(*at):
+        return remote(own.at[at], out.at[at], OUT, OUT, 0, (before, ha, wa))
+
+    def kv_row(row, c):
+        return pl.ds(1, 2), slice(None), row, slice(None), slice(None), lanes(c)
 
     def if_(cond, action):
         pl.when(cond)(action)
@@ -183,13 +187,11 @@
         for side in (0, 1):
             if_(has[side] & rim & keys_move(c), lambda: action(side))
 
-    def stage_send(c, y, z, keys):
-        if y:
-            y_kv(c).start()
-        if z:
-            leaving(c, lambda side, both: z_q(side, c, both).start())
-        if keys:
-            keys_leave(c, lambda side: ext(side, c).start())
+    def queries_send(c):
+        leaving(c, lambda side, both: z_q(side, c, both).start())
+
+    def keys_send(c):
+        keys_leave(c, lambda side: ext(side, c).start())
 
     def passes_corner(c):
         return (by_rim[0] | by_rim[1]) & keys_move(c)
@@ -342,6 +344,7 @@
         py_send[:, :, :, :, ch] = acc[:, :, rows].astype(BF16)
         y_part(c).start()
         own[1:3, :, :, :, :, ch] = acc[:, :, 0:rows].astype(BF16)
+        if_(jnp.logical_not(passes_corner(c)), lambda: result(*kv_row(inner, c)).start())
 
     def sent(c):
         y_kv(c).wait_send()
@@ -364,26 +367,31 @@
 
     def stage_fold(c):
         ch = lanes(c)
-        total[...] = own[:, :, :, :, :, ch].astype(F32)
+        y_part(c).wait_recv()
+        total_kv[...] = own[1:3, :, edge, :, :, ch].astype(F32) + py_recv[:, :, :, :, ch].astype(F32)
 
         def fold(side):
             ext_part(1 - side, c).wait_recv()
             corner_part(1 - side, c).wait_recv()
-            total[1:3, :, :, near[side]] += pz_recv[:, :, :, :, ch].astype(F32)
-            total[1:3, :, edge, near[side]] += pc_recv[:, :, :, ch].astype(F32)
+            total_kv[:, :, near[side]] += (
+                pz_recv[:, :, edge, :, ch].astype(F32) + pc_recv[:, :, :, ch].astype(F32))
+            own[1:3, :, inner, near[side], :, ch] = (
+                own[1:3, :, inner, near[side], :, ch].astype(F32) + pz_recv[:, :, inner, :, ch].astype(F32)).astype(BF16)
+            result(*kv_row(inner, c)).start()
 
         keys_leave(c, fold)
-        y_part(c).wait_recv()
-        total[1:3, :, edge] += py_recv[:, :, :, :, ch].astype(F32)
+        own[1:3, :, edge, :, :, ch] = total_kv[...].astype(BF16)
+        result(*kv_row(edge, c)).start()
+        total_q[...] = own[0, :, :, :, :, ch].astype(F32)
 
         def back(side, both):
             dq_back(1 - side, c, both).wait_recv()
             for col in (range(cols) if both else (near[side],)):
-                total[0, :, :, col] += dqz_recv[side, :, :, col, :, ch].astype(F32)
+                total_q[:, :, col] += dqz_recv[side, :, :, col, :, ch].astype(F32)
 
         leaving(c, back)
-        own[:, :, :, :, :, ch] = total[...].astype(BF16)
-        result(ch).start()
+        own[0, :, :, :, :, ch] = total_q[...].astype(BF16)
+        result(0, slice(None), slice(None), slice(None), slice(None), ch).start()
         sent(c)
 
     def first_copy(side):
@@ -396,8 +404,12 @@
 
     for load in loads:
         load.wait()
-    for c in range(max(AHEAD_Y, AHEAD_Q, AHEAD_E)):
-        stage_send(c, c < AHEAD_Y, c < AHEAD_Q, c < AHEAD_E)
+    ahead_q, ahead_e = (jnp.where(lax.rem(sec, 2) == 0, a, b) for a, b in (AHEAD_Q, AHEAD_E))
+    for c in range(max(AHEAD_Y, *AHEAD_Q, *AHEAD_E)):
+        if c < AHEAD_Y:
+            y_kv(c).start()
+        if_(c < ahead_q, lambda: queries_send(c))
+        if_(c < ahead_e, lambda: keys_send(c))
 
     def window(ref, begin):
         per_t = (rows + 1) * tok
@@ -418,9 +430,9 @@
         if_(has[side], _)
 
     def step(i, carry):
-        if_(i + AHEAD_Y < chunks, lambda: stage_send(i + AHEAD_Y, True, False, False))
-        if_(i + AHEAD_Q < chunks, lambda: stage_send(i + AHEAD_Q, False, True, False))
-        if_(i + AHEAD_E < chunks, lambda: stage_send(i + AHEAD_E, False, False, True))
+        if_(i + AHEAD_Y < chunks, lambda: y_kv(i + AHEAD_Y).start())
+        if_(i + ahead_q < chunks, lambda: queries_send(i + ahead_q))
+        if_(i + ahead_e < chunks, lambda: keys_send(i + ahead_e))
         if_(i + CORNERS_AHEAD < chunks, lambda: stage_corner(i + CORNERS_AHEAD))
         if_(i < chunks, lambda: stage_first(i))
         if_((i >= STAT_LAG) & (i < chunks + STAT_LAG), lambda: stage_second(i - STAT_LAG))
@@ -428,7 +440,7 @@
         return carry
 
     lax.fori_loop(0, chunks + FOLD_LAG, step, 0)
-    result(slice(None)).wait()
+    result().wait()
     for side in (0, 1):
         if_(has[side], lambda: first_copy(side).wait_send())
 
@@ -441,7 +453,7 @@
     width = HEADS_PER_CHUNK * HEAD_DIM
     assert channels % width == 0
     chunks = channels // width
-    assert chunks >= max(AHEAD_Y, AHEAD_Q, AHEAD_E) and AHEAD_Y >= CORNERS_AHEAD
+    assert chunks >= max(AHEAD_Y, *AHEAD_Q, *AHEAD_E) and AHEAD_Y >= CORNERS_AHEAD
     per_col, per_key = grid_t * rows * tok, grid_t * (rows + 1) * tok
     n_q = cols * per_col
     slots = (STAT_LAG + 1) * HEADS_PER_CHUNK
@@ -479,7 +491,8 @@
             vmem((2, grid_t, cols, tok, channels), BF16),
             vmem((2, grid_t, cols, tok, channels), BF16),
             vmem((3,) + q.shape, BF16),
-            vmem((3, grid_t, rows, cols, tok, width), F32),
+            vmem((grid_t, rows, cols, tok, width), F32),
+            vmem((2, grid_t, cols, tok, width), F32),
             pltpu.SemaphoreType.DMA((KINDS, chunks)),
             pltpu.SemaphoreType.DMA((KINDS, chunks)),
         ],

time: 88.7 us -> 87.9 us (level)
  no operation moved by 1% of the time
where the time goes in v3:
time: 87.9 us; the launch traced here: 87.8 us
  Pallas kernels  85.8 us (98%)
  local copies, waits for them, and re-layouts  1.93 us (2%)
    pallas_call x1, Pallas kernels, local(): pl.pallas_call(functools.partial(kernel, (n_sec, n_ha, n_wa, chunks, widt...  85.8 us
    unnamed x1, local copies, waits for them, and re-layouts  1.93 us

profile of v3, /device:TPU:17, one launch (start us, length us, event | category | flops | bytes accessed | tf_op | source)
XLA Modules:
  0.0 87.8 jit_solution(3121199840366276722)
XLA Ops:
  0.0 85.8 %shard_map.46 = bf16[3,4,2,2,16,2560]{5,4,3,2,1,0:T(8,128)(2,1)S(1)} custom-call(s32[2,2,4]{2,1,0:T(2,128)} %bitcast.11, bf16[4,2,2,16,2560]{4,3,2,1,0:T(8,128)(2,1)} %bitcast.9, bf16[2,4,2,2,16,2560]{5,4,3,2,1,0:T(8,128)(2,1)} %bitcast.8, bf16[4,2,2,16,2560]{4,3,2,1,0:T(8,128)(2,1)} %bitcast.10), custom_call_target="tpu_custom_call" | custom-call | tf_op jit(solution)/shard_map/pallas_call | solution.py:462
  85.9 1.9 %copy.7 = bf16[3,1,4,2,2,16,2560]{6,5,4,3,2,1,0:T(8,128)(2,1)} copy(bf16[3,1,4,2,2,16,2560]{6,5,4,3,2,1,0:T(8,128)(2,1)S(1)} %bitcast.7) | data formatting | bytes 7864320

commit v4 on v3

--- a/solution.py
+++ b/solution.py
@@ -13,15 +13,17 @@
 F32 = jnp.float32
 BF16 = jnp.bfloat16
 
-Y_KV, Z_Q, EXT, CORNER, STAT, DQ, EXT_PART, CORNER_PART, Y_PART, OUT, KINDS = (
-    0, 1, 3, 4, 5, 7, 9, 10, 11, 12, 13)
+Y_KV, Z_Q, EXT, CORNER, STAT, DQ, EXT_INNER, EXT_EDGE, CORNER_PART, Y_PART, OUT, SHIFT, KINDS = (
+    0, 1, 3, 4, 5, 7, 9, 10, 11, 12, 13, 14, 15)
 
 AHEAD_Y = 6
 AHEAD_Q = 3, 3
 AHEAD_E = 3, 3
 CORNERS_AHEAD = 2
 STAT_LAG = 2
-FOLD_LAG = 4
+MERGE_LAG = 3
+FOLD_LAG = 5
+SHIFTED = 6
 LOW = -1e30
 VMEM_KIB = 56000
 
@@ -58,8 +60,15 @@
     by_rim = (wa == 1, wa == n_wa - 2)
     scale = HEAD_DIM ** (-0.5)
 
-    loads = [pltpu.make_async_copy(src, dst, load_sem.at[n]) for n, (src, dst) in enumerate(
-        ((q_in, qg.at[0]), (go_in, qg.at[1]), (kv_in, kx.at[:, :, 0:rows, 0:cols])))]
+    staying = chunks - SHIFTED
+    kept, moved_on = slice(0, staying * width), slice(staying * width, chunks * width)
+
+    def held(at):
+        return ((q_in, qg.at[0, :, :, :, :, at]), (go_in, qg.at[1, :, :, :, :, at]),
+                (kv_in, kx.at[:, :, 0:rows, 0:cols, :, at]))
+
+    loads = [pltpu.make_async_copy(src.at[(slice(None),) * (len(src.shape) - 1) + (kept,)], dst, load_sem.at[n])
+             for n, (src, dst) in enumerate(held(kept))]
     for load in loads:
         load.start()
 
@@ -86,16 +95,11 @@
         def _():
             greet(sec, ha, peer[side])
 
-        @pl.when(has[side] & (rim | by_rim[side]))
-        def _():
-            greet(sec, other, peer[side])
-
     sides_here = jnp.minimum(wa, 1) + jnp.minimum(n_wa - 1 - wa, 1)
-    rims_here = jnp.where(rim, 1, by_rim[0].astype(jnp.int32) + by_rim[1].astype(jnp.int32))
-    pl.semaphore_wait(barrier, 3 + sides_here + rims_here)
+    pl.semaphore_wait(barrier, 3 + sides_here)
 
     def keys_move(c):
-        return ((lax.rem(c, 5) == 2) | (lax.rem(c, 5) == 0)) & (c > 0) & (c < chunks - 2)
+        return (lax.rem(c, 3) == 2) & (c < chunks - 2)
 
     def lanes(c):
         return pl.ds(pl.multiple_of(c * width, width), width)
@@ -110,6 +114,9 @@
         return pltpu.make_async_remote_copy(
             src_ref=src, dst_ref=dst, send_sem=send_sem.at[sent, c], recv_sem=recv_sem.at[arrived, c],
             device_id=device, device_id_type=MESH)
+
+    shifts = [remote(src.at[(slice(None),) * (len(src.shape) - 1) + (moved_on,)], dst, SHIFT, SHIFT, n, (before, ha, wa))
+              for n, (src, dst) in enumerate(held(moved_on))]
 
     def y_kv(c):
         return remote(kx.at[:, :, edge, 0:cols, :, lanes(c)], kx.at[:, :, rows, 0:cols, :, lanes(c)],
@@ -139,13 +146,17 @@
         return remote(dqz_send.at[side, :, :, at, :, lanes(c)], dqz_recv.at[1 - side, :, :, at, :, lanes(c)],
                       DQ + side, DQ + 1 - side, c, (sec, ha, peer[side]))
 
-    def ext_part(side, c):
-        return remote(pz_send.at[:, :, 0:rows, :, lanes(c)], pz_recv.at[:, :, :, :, lanes(c)],
-                      EXT_PART, EXT_PART, c, (sec, ha, peer[side]))
-
-    def corner_part(side, c):
+    def ext_inner(side, c):
+        return remote(pz_send.at[:, :, inner, :, lanes(c)], pz_recv.at[:, :, inner, :, lanes(c)],
+                      EXT_INNER, EXT_INNER, c, (sec, ha, peer[side]))
+
+    def ext_edge(side, c):
+        return remote(pz_send.at[:, :, edge, :, lanes(c)], pz_recv.at[:, :, edge, :, lanes(c)],
+                      EXT_EDGE, EXT_EDGE, c, (sec, ha, peer[side]))
+
+    def corner_part(c):
         return remote(pz_send.at[:, :, rows, :, lanes(c)], pc_recv.at[:, :, :, lanes(c)],
-                      CORNER_PART, CORNER_PART, c, (sec, other, peer[side]))
+                      CORNER_PART, CORNER_PART, c, (sec, other, wa))
 
     def y_part(c):
         return remote(py_send.at[:, :, :, :, lanes(c)], py_recv.at[:, :, :, :, lanes(c)],
@@ -330,8 +341,8 @@
         if_(jnp.logical_not(far), lambda: heads(lambda j: own_second(cols, c, j)))
 
         def extra(side):
-            ext_part(side, c).start()
-            corner_part(side, c).start()
+            ext_inner(side, c).start()
+            corner_part(c).start()
 
         keys_come(c, extra)
 
@@ -344,7 +355,7 @@
         py_send[:, :, :, :, ch] = acc[:, :, rows].astype(BF16)
         y_part(c).start()
         own[1:3, :, :, :, :, ch] = acc[:, :, 0:rows].astype(BF16)
-        if_(jnp.logical_not(passes_corner(c)), lambda: result(*kv_row(inner, c)).start())
+        if_(jnp.logical_not(passes_corner(c)) & (c < staying), lambda: result(*kv_row(inner, c)).start())
 
     def sent(c):
         y_kv(c).wait_send()
@@ -357,31 +368,42 @@
         keys_leave(c, keys_sent)
 
         def extra_sent(side):
-            ext_part(side, c).wait_send()
-            corner_part(side, c).wait_send()
+            ext_inner(side, c).wait_send()
+            ext_edge(side, c).wait_send()
+            corner_part(c).wait_send()
 
         keys_come(c, extra_sent)
         exchanged(c, lambda side, both: stat(side, c, both).wait_send())
         coming(c, lambda side, both: dq_back(side, c, both).wait_send())
         y_part(c).wait_send()
 
+    def stage_merge(c):
+        ch = lanes(c)
+
+        def merged(side):
+            corner_part(c).wait_recv()
+            pz_send[:, :, edge, :, ch] = (
+                pz_send[:, :, edge, :, ch].astype(F32) + pc_recv[:, :, :, ch].astype(F32)).astype(BF16)
+            ext_edge(side, c).start()
+
+        keys_come(c, merged)
+
     def stage_fold(c):
         ch = lanes(c)
         y_part(c).wait_recv()
         total_kv[...] = own[1:3, :, edge, :, :, ch].astype(F32) + py_recv[:, :, :, :, ch].astype(F32)
 
         def fold(side):
-            ext_part(1 - side, c).wait_recv()
-            corner_part(1 - side, c).wait_recv()
-            total_kv[:, :, near[side]] += (
-                pz_recv[:, :, edge, :, ch].astype(F32) + pc_recv[:, :, :, ch].astype(F32))
+            ext_edge(1 - side, c).wait_recv()
+            total_kv[:, :, near[side]] += pz_recv[:, :, edge, :, ch].astype(F32)
+            ext_inner(1 - side, c).wait_recv()
             own[1:3, :, inner, near[side], :, ch] = (
                 own[1:3, :, inner, near[side], :, ch].astype(F32) + pz_recv[:, :, inner, :, ch].astype(F32)).astype(BF16)
-            result(*kv_row(inner, c)).start()
+            if_(c < staying, lambda: result(*kv_row(inner, c)).start())
 
         keys_leave(c, fold)
         own[1:3, :, edge, :, :, ch] = total_kv[...].astype(BF16)
-        result(*kv_row(edge, c)).start()
+        if_(c < staying, lambda: result(*kv_row(edge, c)).start())
         total_q[...] = own[0, :, :, :, :, ch].astype(F32)
 
         def back(side, both):
@@ -390,8 +412,17 @@
                 total_q[:, :, col] += dqz_recv[side, :, :, col, :, ch].astype(F32)
 
         leaving(c, back)
-        own[0, :, :, :, :, ch] = total_q[...].astype(BF16)
-        result(0, slice(None), slice(None), slice(None), slice(None), ch).start()
+
+        def leave():
+            own[0, :, :, :, :, ch] = total_q[...].astype(BF16)
+            result(0, slice(None), slice(None), slice(None), slice(None), ch).start()
+
+        def stay():
+            out[0, :, :, :, :, ch] = total_q[...].astype(BF16)
+            out[1:3, :, :, :, :, ch] = own[1:3, :, :, :, :, ch]
+
+        if_(c < staying, leave)
+        if_(c >= staying, stay)
         sent(c)
 
     def first_copy(side):
@@ -402,6 +433,8 @@
     for side in (0, 1):
         if_(has[side], lambda: first_copy(side).start())
 
+    for shift in shifts:
+        shift.start()
     for load in loads:
         load.wait()
     ahead_q, ahead_e = (jnp.where(lax.rem(sec, 2) == 0, a, b) for a, b in (AHEAD_Q, AHEAD_E))
@@ -430,17 +463,25 @@
         if_(has[side], _)
 
     def step(i, carry):
+        def arrived():
+            for shift in shifts:
+                shift.wait_recv()
+
+        if_(i + AHEAD_Y == staying, arrived)
         if_(i + AHEAD_Y < chunks, lambda: y_kv(i + AHEAD_Y).start())
         if_(i + ahead_q < chunks, lambda: queries_send(i + ahead_q))
         if_(i + ahead_e < chunks, lambda: keys_send(i + ahead_e))
         if_(i + CORNERS_AHEAD < chunks, lambda: stage_corner(i + CORNERS_AHEAD))
         if_(i < chunks, lambda: stage_first(i))
         if_((i >= STAT_LAG) & (i < chunks + STAT_LAG), lambda: stage_second(i - STAT_LAG))
+        if_((i >= MERGE_LAG) & (i < chunks + MERGE_LAG), lambda: stage_merge(i - MERGE_LAG))
         if_(i >= FOLD_LAG, lambda: stage_fold(i - FOLD_LAG))
         return carry
 
     lax.fori_loop(0, chunks + FOLD_LAG, step, 0)
-    result().wait()
+    result(slice(None), slice(None), slice(None), slice(None), slice(None), kept).wait()
+    for shift in shifts:
+        shift.wait_send()
     for side in (0, 1):
         if_(has[side], lambda: first_copy(side).wait_send())
 
@@ -454,6 +495,7 @@
     assert channels % width == 0
     chunks = channels // width
     assert chunks >= max(AHEAD_Y, *AHEAD_Q, *AHEAD_E) and AHEAD_Y >= CORNERS_AHEAD
+    assert AHEAD_Y >= max(*AHEAD_Q, *AHEAD_E) and chunks - SHIFTED >= AHEAD_Y and SHIFTED > 0
     per_col, per_key = grid_t * rows * tok, grid_t * (rows + 1) * tok
     n_q = cols * per_col
     slots = (STAT_LAG + 1) * HEADS_PER_CHUNK

time: 87.9 us -> 81.4 us (0.926)
  the two profiles are of different devices: /device:TPU:17 before, /device:TPU:0 now
where the time goes in v4:
time: 81.4 us; the launch traced here: 81.2 us
  Pallas kernels  79.3 us (97%)
  local copies, waits for them, and re-layouts  1.93 us (2%)
    pallas_call x1, Pallas kernels, local(): pl.pallas_call(functools.partial(kernel, (n_sec, n_ha, n_wa, chunks, widt...  79.3 us
    unnamed x1, local copies, waits for them, and re-layouts  1.93 us

profile of v4, /device:TPU:0, one launch (start us, length us, event | category | flops | bytes accessed | tf_op | source)
XLA Modules:
  0.0 81.2 jit_solution(4862697469024795977)
XLA Ops:
  0.0 79.3 %shard_map.46 = bf16[3,4,2,2,16,2560]{5,4,3,2,1,0:T(8,128)(2,1)S(1)} custom-call(s32[2,2,4]{2,1,0:T(2,128)} %bitcast.11, bf16[4,2,2,16,2560]{4,3,2,1,0:T(8,128)(2,1)} %bitcast.9, bf16[2,4,2,2,16,2560]{5,4,3,2,1,0:T(8,128)(2,1)} %bitcast.8, bf16[4,2,2,16,2560]{4,3,2,1,0:T(8,128)(2,1)} %bitcast.10), custom_call_target="tpu_custom_call" | custom-call | tf_op jit(solution)/shard_map/pallas_call | solution.py:504
  79.3 1.9 %copy.7 = bf16[3,1,4,2,2,16,2560]{6,5,4,3,2,1,0:T(8,128)(2,1)} copy(bf16[3,1,4,2,2,16,2560]{6,5,4,3,2,1,0:T(8,128)(2,1)S(1)} %bitcast.7) | data formatting | bytes 7864320

commit v5 on v4

--- a/solution.py
+++ b/solution.py
@@ -21,9 +21,9 @@
 AHEAD_E = 3, 3
 CORNERS_AHEAD = 2
 STAT_LAG = 2
-MERGE_LAG = 3
+MERGE_LAG = 4
 FOLD_LAG = 5
-SHIFTED = 6
+SHIFTED = 7
 LOW = -1e30
 VMEM_KIB = 56000
 
@@ -473,8 +473,8 @@
         if_(i + ahead_e < chunks, lambda: keys_send(i + ahead_e))
         if_(i + CORNERS_AHEAD < chunks, lambda: stage_corner(i + CORNERS_AHEAD))
         if_(i < chunks, lambda: stage_first(i))
+        if_((i >= MERGE_LAG) & (i < chunks + MERGE_LAG), lambda: stage_merge(i - MERGE_LAG))
         if_((i >= STAT_LAG) & (i < chunks + STAT_LAG), lambda: stage_second(i - STAT_LAG))
-        if_((i >= MERGE_LAG) & (i < chunks + MERGE_LAG), lambda: stage_merge(i - MERGE_LAG))
         if_(i >= FOLD_LAG, lambda: stage_fold(i - FOLD_LAG))
         return carry
 

time: 81.4 us -> 80.7 us (level)
  no operation moved by 1% of the time
where the time goes in v5:
time: 80.7 us; the launch traced here: 80.6 us
  Pallas kernels  78.6 us (97%)
  local copies, waits for them, and re-layouts  1.93 us (2%)
    pallas_call x1, Pallas kernels, local(): pl.pallas_call(functools.partial(kernel, (n_sec, n_ha, n_wa, chunks, widt...  78.6 us
    unnamed x1, local copies, waits for them, and re-layouts  1.93 us

profile of v5, /device:TPU:0, one launch (start us, length us, event | category | flops | bytes accessed | tf_op | source)
XLA Modules:
  0.0 80.6 jit_solution(4082433594610894338)
XLA Ops:
  0.0 78.6 %shard_map.46 = bf16[3,4,2,2,16,2560]{5,4,3,2,1,0:T(8,128)(2,1)S(1)} custom-call(s32[2,2,4]{2,1,0:T(2,128)} %bitcast.11, bf16[4,2,2,16,2560]{4,3,2,1,0:T(8,128)(2,1)} %bitcast.9, bf16[2,4,2,2,16,2560]{5,4,3,2,1,0:T(8,128)(2,1)} %bitcast.8, bf16[4,2,2,16,2560]{4,3,2,1,0:T(8,128)(2,1)} %bitcast.10), custom_call_target="tpu_custom_call" | custom-call | tf_op jit(solution)/shard_map/pallas_call | solution.py:504
  78.7 1.9 %copy.7 = bf16[3,1,4,2,2,16,2560]{6,5,4,3,2,1,0:T(8,128)(2,1)} copy(bf16[3,1,4,2,2,16,2560]{6,5,4,3,2,1,0:T(8,128)(2,1)S(1)} %bitcast.7) | data formatting | bytes 7864320

commit v6 on v5

--- a/solution.py
+++ b/solution.py
@@ -16,7 +16,7 @@
 Y_KV, Z_Q, EXT, CORNER, STAT, DQ, EXT_INNER, EXT_EDGE, CORNER_PART, Y_PART, OUT, SHIFT, KINDS = (
     0, 1, 3, 4, 5, 7, 9, 10, 11, 12, 13, 14, 15)
 
-AHEAD_Y = 6
+AHEAD_Y = 5
 AHEAD_Q = 3, 3
 AHEAD_E = 3, 3
 CORNERS_AHEAD = 2
@@ -433,8 +433,6 @@
     for side in (0, 1):
         if_(has[side], lambda: first_copy(side).start())
 
-    for shift in shifts:
-        shift.start()
     for load in loads:
         load.wait()
     ahead_q, ahead_e = (jnp.where(lax.rem(sec, 2) == 0, a, b) for a, b in (AHEAD_Q, AHEAD_E))
@@ -443,6 +441,8 @@
             y_kv(c).start()
         if_(c < ahead_q, lambda: queries_send(c))
         if_(c < ahead_e, lambda: keys_send(c))
+    for shift in shifts:
+        shift.start()
 
     def window(ref, begin):
         per_t = (rows + 1) * tok

time: 80.7 us -> 80.7 us (level)
  no operation moved by 1% of the time
where the time goes in v6:
time: 80.7 us; the launch traced here: 80.6 us
  Pallas kernels  78.6 us (97%)
  local copies, waits for them, and re-layouts  1.93 us (2%)
    pallas_call x1, Pallas kernels, local(): pl.pallas_call(functools.partial(kernel, (n_sec, n_ha, n_wa, chunks, widt...  78.6 us
    unnamed x1, local copies, waits for them, and re-layouts  1.93 us

profile of v6, /device:TPU:0, one launch (start us, length us, event | category | flops | bytes accessed | tf_op | source)
XLA Modules:
  0.0 80.6 jit_solution(16152008700970272751)
XLA Ops:
  0.0 78.6 %shard_map.46 = bf16[3,4,2,2,16,2560]{5,4,3,2,1,0:T(8,128)(2,1)S(1)} custom-call(s32[2,2,4]{2,1,0:T(2,128)} %bitcast.11, bf16[4,2,2,16,2560]{4,3,2,1,0:T(8,128)(2,1)} %bitcast.9, bf16[2,4,2,2,16,2560]{5,4,3,2,1,0:T(8,128)(2,1)} %bitcast.8, bf16[4,2,2,16,2560]{4,3,2,1,0:T(8,128)(2,1)} %bitcast.10), custom_call_target="tpu_custom_call" | custom-call | tf_op jit(solution)/shard_map/pallas_call | solution.py:504
  78.7 1.9 %copy.7 = bf16[3,1,4,2,2,16,2560]{6,5,4,3,2,1,0:T(8,128)(2,1)} copy(bf16[3,1,4,2,2,16,2560]{6,5,4,3,2,1,0:T(8,128)(2,1)S(1)} %bitcast.7) | data formatting | bytes 7864320
